TPU v7x, 32 devices: a whole 2x2x4 slice. The times are simulated.
32 devices in a mesh: seq: 16 (over z, y, core), mp: 2 (over x).
Axes of the slice: x: 2, y: 2, z: 4, core: 2. Of those that a mesh axis runs over, the one named last changes fastest.
Arguments:
- hidden: bfloat16 [4096, 2048], P('seq'), may hold values from -6 to 6
- ids: int32 [4096], P('seq'), may hold values from 0 to 4, as said below
- w_value: bfloat16 [2048, 2048], P(None, 'mp'), may hold values from -0.125 to 0.125
- w_bc: bfloat16 [2048, 2, 64], P(None, 'mp'), may hold values from -0.015625 to 0.015625
- w_step: bfloat16 [2048, 16], P(None, 'mp'), may hold values from -0.125 to 0.125
- step_bias: float32 [16], P('mp'), may hold values from -1 to 1
- decay_log: float32 [16], P('mp'), may hold values from -12 to -2
- skip: float32 [16], P('mp'), may hold values from 0.5 to 1.5
- norm_gain: float32 [2048], P('mp'), may hold values from 0.1 to 1.9
- w_out: bfloat16 [2048, 2048], P('mp'), may hold values from -0.125 to 0.125
- cotangent: bfloat16 [4096, 2048], P('seq'), may hold values from -6 to 6
Outputs:
- out: bfloat16 [4096, 2048], P('seq', 'mp')
- d_hidden: bfloat16 [4096, 2048], P('seq', 'mp')
Inputs may be any that keep to these rules, and one draw needn't show every extreme that they name: `ids`: 4 marks an unknown base (N); such bases come in runs.
All inputs are finite; a program needn't handle non-finite values.
Results may differ from a plain program's by a relative error of at most 0.014.
Values may be sent and summed in bfloat16 or wider, within the bound.
A program may use at most 320 MiB of HBM per device.

v0:
```python
from functools import partial

import jax
import jax.numpy as jnp
from jax import lax
from jax.experimental import pallas as pl
from jax.experimental.pallas import tpu as pltpu
from jax.sharding import PartitionSpec as P

f32, bf16 = jnp.float32, jnp.bfloat16
epsilon = 1e-05
LANES = 128
MXU_NN = (((1,), (0,)), ((), ()))
MXU_NT = (((1,), (1,)), ((), ()))
MXU_TN = (((0,), (0,)), ((), ()))
PARAMS = pltpu.CompilerParams(vmem_limit_bytes=56 * 1024 * 1024)


def dot(a, b, dims=MXU_NN, precision=None):
    return lax.dot_general(a, b, dims, preferred_element_type=f32, precision=precision)


def iota2(shape, axis):
    return lax.broadcasted_iota(jnp.int32, shape, axis)


def exchange_matrix():
    return (iota2((LANES, LANES), 0) + iota2((LANES, LANES), 1) == LANES - 1).astype(bf16)


def sources_kernel(hidden_ref, cot_ref, ids_ref, src_ref, grad_ref):
    tiles = hidden_ref.shape[1] // LANES
    mirror = exchange_matrix()
    known = ids_ref[...] != 4
    src_ref[0] = hidden_ref[...]
    for k in range(tiles):
        there = pl.ds((tiles - 1 - k) * LANES, LANES)
        here = pl.ds(k * LANES, LANES)
        src_ref[1, :, there] = dot(hidden_ref[:, here], mirror).astype(bf16)
        tile = jnp.where(known, cot_ref[:, here].astype(f32), 0.0).astype(bf16)
        grad_ref[0, :, here] = tile
        grad_ref[1, :, there] = dot(tile, mirror).astype(bf16)


def merge_kernel(terms_ref, out_ref):
    parts, _, width = out_ref.shape
    tiles = parts * width // LANES
    per = width // LANES
    mirror = exchange_matrix()
    for k in range(tiles):
        back = tiles - 1 - k
        flipped = dot(terms_ref[1, :, pl.ds(back * LANES, LANES)].astype(bf16), mirror)
        out_ref[k // per, :, pl.ds((k % per) * LANES, LANES)] = (
            terms_ref[0, :, pl.ds(k * LANES, LANES)] + flipped
        )


def prepare(aux, consts):
    length = aux.shape[0]
    shifted = aux + consts[0:1]
    dt = jnp.maximum(shifted, 0.0) + jnp.log1p(jnp.exp(-jnp.abs(shifted)))
    la = -jnp.exp(consts[1:2]) * dt
    lower = (iota2((length, length), 0) >= iota2((length, length), 1)).astype(f32)
    cum = dot(lower, la, precision=lax.Precision.HIGHEST)
    return shifted, dt, la, cum, cum - la


def ends_kernel(heads, state, aux_ref, consts_ref, x_ref, st_ref, dec_ref):
    aux = aux_ref[0]
    length = aux.shape[0]
    _, dt, la, cum, exc = prepare(aux, consts_ref[...])
    cum_t, exc_t, dt_t = cum.T[:heads], exc.T[:heads], dt.T[:heads]
    b_t = aux.astype(bf16).astype(f32).T[LANES - 2 * state : LANES - state]
    end = cum_t[:, length - 1 : length]
    w_f = jnp.exp(end - cum_t) * dt_t
    w_r = jnp.exp(exc_t) * dt_t
    for h in range(heads):
        left = jnp.concatenate([b_t * w_f[h : h + 1], b_t * w_r[h : h + 1]], axis=0).astype(bf16)
        both = dot(left, x_ref[0, :, pl.ds(h * LANES, LANES)]).astype(bf16)
        st_ref[0, 0, h] = both[:state]
        st_ref[0, 1, h] = both[state:]
    dec_ref[0] = jnp.broadcast_to(end, (heads, LANES))


def carried(me, count, all_ref, dec_ref, which, upward):
    shape = all_ref.shape[3:]

    def step(i, total):
        j = (count - 1 - i) if upward else i
        return jnp.exp(dec_ref[j, 0])[:, None, :] * total + all_ref[j, 0, which].astype(f32)

    steps = (count - 1 - me) if upward else me
    return lax.fori_loop(0, steps, step, jnp.zeros(shape, f32))


def outputs_kernel(
    heads, state, count,
    me_ref, aux_ref, consts_ref, x_ref, dz_ref, gain_ref, st_ref, dec_ref,
    z_ref, dy_ref, adj_ref, start_ref, y_scr,
):
    aux, consts = aux_ref[0], consts_ref[...]
    length = aux.shape[0]
    me = me_ref[0]
    _, dt, la, cum, exc = prepare(aux, consts)
    cum_t, exc_t, dt_t = cum.T[:heads], exc.T[:heads], dt.T[:heads]
    end_t = cum_t[:, length - 1 : length]
    rounded = aux.astype(bf16)
    b_m = rounded[:, LANES - 2 * state : LANES - state]
    c_m = rounded[:, LANES - state :]
    c32 = c_m.astype(f32)
    c_t = rounded.astype(f32).T[LANES - state :]
    start_ref[0, 0] = carried(me, count, st_ref, dec_ref, 0, False)
    start_ref[0, 1] = carried(me, count, st_ref, dec_ref, 1, True)
    scores = dot(c_m, b_m, MXU_NT)
    rows, cols = iota2((length, length), 0), iota2((length, length), 1)
    grow_f = jnp.exp(cum)
    grow_r = jnp.exp(cum[length - 1 : length] - exc)
    sq_f = jnp.zeros((length, 1), f32)
    sq_r = jnp.zeros((length, 1), f32)
    for h in range(heads):
        at = pl.ds(h * LANES, LANES)
        one = slice(h, h + 1)
        spread = jnp.where(
            rows >= cols, cum[:, one] - cum_t[one], exc_t[one] - exc[:, one]
        )
        mix = jnp.exp(spread) * scores * dt_t[one]
        low = jnp.where(rows >= cols, mix, 0.0).astype(bf16)
        high = jnp.where(rows <= cols, mix, 0.0).astype(bf16)
        x_h = x_ref[0, :, at]
        direct = consts[2:3, one] * x_h.astype(f32)
        y_f = dot(low, x_h) + direct
        y_f += dot((c32 * grow_f[:, one]).astype(bf16), start_ref[0, 0, h].astype(bf16))
        y_r = dot(high, x_h) + direct
        y_r += dot((c32 * grow_r[:, one]).astype(bf16), start_ref[0, 1, h].astype(bf16))
        y_scr[0, :, at] = y_f
        y_scr[1, :, at] = y_r
        sq_f += jnp.sum(y_f * y_f, axis=1, keepdims=True)
        sq_r += jnp.sum(y_r * y_r, axis=1, keepdims=True)
    share = 1.0 / (heads * LANES)
    rs_f = lax.rsqrt(sq_f * share + epsilon)
    rs_r = lax.rsqrt(sq_r * share + epsilon)
    m_f = jnp.zeros((length, 1), f32)
    m_r = jnp.zeros((length, 1), f32)
    for h in range(heads):
        at = pl.ds(h * LANES, LANES)
        gain = gain_ref[:, at]
        n_f, n_r = y_scr[0, :, at] * rs_f, y_scr[1, :, at] * rs_r
        z_ref[0, :, at] = (n_f * gain + n_r * gain).astype(bf16)
        g = dz_ref[0, :, at].astype(f32) * gain
        m_f += jnp.sum(g * n_f, axis=1, keepdims=True)
        m_r += jnp.sum(g * n_r, axis=1, keepdims=True)
    m_f, m_r = m_f * share, m_r * share
    out_f = jnp.exp(cum_t)
    out_r = jnp.exp(end_t - exc_t)
    for h in range(heads):
        at = pl.ds(h * LANES, LANES)
        one = slice(h, h + 1)
        g = dz_ref[0, :, at].astype(f32) * gain_ref[:, at]
        d_f = (rs_f * (g - y_scr[0, :, at] * rs_f * m_f)).astype(bf16)
        d_r = (rs_r * (g - y_scr[1, :, at] * rs_r * m_r)).astype(bf16)
        dy_ref[0, 0, :, at] = d_f
        dy_ref[0, 1, :, at] = d_r
        adj_ref[0, 0, h] = dot((c_t * out_f[one]).astype(bf16), d_f).astype(bf16)
        adj_ref[0, 1, h] = dot((c_t * out_r[one]).astype(bf16), d_r).astype(bf16)


def grads_kernel(
    heads, state, count,
    me_ref, aux_ref, consts_ref, x_ref, dy_ref, start_ref, own_ref, adj_ref, dec_ref,
    dx_ref, tail_ref, in_scr,
):
    aux, consts = aux_ref[0], consts_ref[...]
    length = aux.shape[0]
    me = me_ref[0]
    shifted, dt, la, cum, exc = prepare(aux, consts)
    cum_t, exc_t = cum.T[:heads], exc.T[:heads]
    end = cum[length - 1 : length]
    rounded = aux.astype(bf16)
    b_m = rounded[:, LANES - 2 * state : LANES - state]
    c_m = rounded[:, LANES - state :]
    b32, c32 = b_m.astype(f32), c_m.astype(f32)
    in_scr[0] = carried(me, count, adj_ref, dec_ref, 0, True)
    in_scr[1] = carried(me, count, adj_ref, dec_ref, 1, False)
    scores_t = dot(b_m, c_m, MXU_NT)
    rows, cols = iota2((length, length), 0), iota2((length, length), 1)
    lane = iota2((length, LANES), 1)
    lane_row = iota2((1, LANES), 1)
    grow_f, grow_r = jnp.exp(cum), jnp.exp(end - exc)
    tail_f, tail_r = jnp.exp(end - cum), jnp.exp(exc)
    end_decay = jnp.exp(end)
    zero = jnp.zeros((length, LANES), f32)
    into_f, into_r = zero, zero
    carry_f, carry_r = zero, zero
    total = jnp.zeros((1, LANES), f32)
    from_f, from_r = [], []
    d_scores = jnp.zeros((length, length), f32)
    d_b = jnp.zeros((length, state), f32)
    d_c = jnp.zeros((length, state), f32)
    for h in range(heads):
        at = pl.ds(h * LANES, LANES)
        one = slice(h, h + 1)
        x_h, d_f, d_r = x_ref[0, :, at], dy_ref[0, 0, :, at], dy_ref[0, 1, :, at]
        s_f, s_r = start_ref[0, 0, h], start_ref[0, 1, h]
        a_f, a_r = in_scr[0, h], in_scr[1, h]
        dt_h = dt[:, one]
        decay = jnp.exp(
            jnp.where(cols >= rows, cum_t[one] - cum[:, one], exc[:, one] - exc_t[one])
        )
        weight = decay * scores_t
        w_f = jnp.where(cols >= rows, weight, 0.0)
        w_r = jnp.where(cols <= rows, weight, 0.0)
        p_f = dot(x_h, d_f, MXU_NT)
        p_r = dot(x_h, d_r, MXU_NT)
        picked = jnp.where(cols >= rows, p_f, 0.0) + jnp.where(cols <= rows, p_r, 0.0)
        d_scores += decay * picked * dt_h
        n_f, n_r = w_f * p_f, w_r * p_r
        from_f.append(jnp.sum(n_f * dt_h, axis=0, keepdims=True))
        from_r.append(jnp.sum(n_r * dt_h, axis=0, keepdims=True))
        in_f = jnp.sum(n_f, axis=1, keepdims=True)
        in_r = jnp.sum(n_r, axis=1, keepdims=True)
        d_u = dot(w_f.astype(bf16), d_f) + dot(w_r.astype(bf16), d_r)
        d_u += dot((b32 * tail_f[:, one]).astype(bf16), a_f.astype(bf16))
        d_u += dot((b32 * tail_r[:, one]).astype(bf16), a_r.astype(bf16))
        v_f = dot(x_h, a_f.astype(bf16), MXU_NT) * tail_f[:, one]
        v_r = dot(x_h, a_r.astype(bf16), MXU_NT) * tail_r[:, one]
        d_b += (v_f + v_r) * dt_h
        in_f += jnp.sum(v_f * b32, axis=1, keepdims=True)
        in_r += jnp.sum(v_r * b32, axis=1, keepdims=True)
        u_f = dot(d_f, s_f.astype(bf16), MXU_NT) * grow_f[:, one]
        u_r = dot(d_r, s_r.astype(bf16), MXU_NT) * grow_r[:, one]
        d_c += u_f + u_r
        c_f = jnp.sum(u_f * c32, axis=1, keepdims=True)
        c_r = jnp.sum(u_r * c32, axis=1, keepdims=True)
        skipped = consts[2:3, one] * (d_f.astype(f32) + d_r.astype(f32))
        dx_ref[0, :, at] = (dt_h * d_u + skipped).astype(bf16)
        into_f = jnp.where(lane == h, in_f, into_f)
        into_r = jnp.where(lane == h, in_r, into_r)
        carry_f = jnp.where(lane == h, c_f, carry_f)
        carry_r = jnp.where(lane == h, c_r, carry_r)
        ending = a_f * (end_decay[:, one] * s_f + own_ref[0, 0, h].astype(f32))
        ending += a_r * (end_decay[:, one] * s_r)
        ended = jnp.sum(jnp.sum(ending, axis=1, keepdims=True), axis=0, keepdims=True)
        ended += jnp.sum(c_r, axis=0, keepdims=True)
        total = jnp.where(lane_row == h, ended, total)
    pad = [jnp.zeros((LANES - heads, length), f32)]
    given_f = jnp.concatenate(from_f + pad, axis=0).T + carry_f
    given_r = jnp.concatenate(from_r + pad, axis=0).T + carry_r
    d_cum = given_f - dt * into_f
    d_exc = dt * into_r - given_r
    upper = (rows <= cols).astype(f32)
    d_la = dot(upper, d_cum + d_exc, precision=lax.Precision.HIGHEST) - d_exc + total
    d_dt = into_f + into_r - jnp.exp(consts[1:2]) * d_la
    d_raw = jnp.where(lane < heads, d_dt * jax.nn.sigmoid(shifted), 0.0)
    d_scores = d_scores.astype(bf16)
    d_b += dot(d_scores, c_m)
    d_c += dot(d_scores, b_m, MXU_TN)
    tail_ref[0] = jnp.concatenate(
        [d_raw[:, : LANES - 2 * state], d_b, d_c], axis=1
    ).astype(bf16)


def by_stream(*shape):
    return pl.BlockSpec((1,) + shape, lambda s: (s,) + (0,) * len(shape))


def gathered(count, *shape):
    return pl.BlockSpec((count, 1) + shape, lambda s: (0, s) + (0,) * len(shape))


def shared(*shape):
    return pl.BlockSpec(shape, lambda s: (0,) * len(shape))


def shape_of(dtype, *shape):
    return jax.ShapeDtypeStruct(shape, dtype)


def join_halves(terms, parts):
    _, length, width = terms.shape
    halves = pl.pallas_call(
        merge_kernel,
        out_shape=shape_of(f32, parts, length, width // parts),
        compiler_params=PARAMS,
    )(terms)
    mine = lax.axis_index("mp")
    own = lax.dynamic_index_in_dim(halves, mine, 0, keepdims=False)
    for hop in range(1, parts):
        there = lax.rem(mine + hop, parts)
        leaving = lax.dynamic_index_in_dim(halves, there, 0, keepdims=False).astype(bf16)
        own += lax.ppermute(
            leaving, "mp", [(i, (i + hop) % parts) for i in range(parts)]
        ).astype(f32)
    return own.astype(bf16)


def per_device(
    hidden, ids, w_value, w_bc, w_step, step_bias, decay_log, skip, norm_gain, w_out, cotangent
):
    length, width = hidden.shape
    heads = w_step.shape[1]
    inner = w_value.shape[1]
    state = w_bc.shape[2] // 2
    assert w_bc.shape[1] == 1 and inner == heads * LANES
    count, parts = lax.axis_size("seq"), lax.axis_size("mp")
    me = lax.axis_index("seq").reshape(1).astype(jnp.int32)
    me_spec = pl.BlockSpec(memory_space=pltpu.SMEM)
    sources, grads = pl.pallas_call(
        sources_kernel,
        out_shape=(shape_of(bf16, 2, length, width),) * 2,
        compiler_params=PARAMS,
    )(hidden, cotangent, ids[:, None])
    sources = sources.reshape(2 * length, width)
    grads = grads.reshape(2 * length, width)
    spare = jnp.zeros((width, LANES - heads - 2 * state), bf16)
    w_side = jnp.concatenate([w_step, spare, w_bc.reshape(width, -1)], axis=1)
    consts = jnp.pad(
        jnp.stack([step_bias, decay_log, skip]), ((0, 5), (0, LANES - heads))
    )
    aux = dot(sources, w_side).reshape(2, length, LANES)
    x = dot(sources, w_value).astype(bf16).reshape(2, length, inner)
    states, decays = pl.pallas_call(
        partial(ends_kernel, heads, state),
        grid=(2,),
        in_specs=[by_stream(length, LANES), shared(8, LANES), by_stream(length, inner)],
        out_specs=[by_stream(2, heads, state, LANES), by_stream(heads, LANES)],
        out_shape=(shape_of(bf16, 2, 2, heads, state, LANES), shape_of(f32, 2, heads, LANES)),
        compiler_params=PARAMS,
    )(aux, consts, x)
    all_states = lax.all_gather(states, "seq")
    all_decays = lax.all_gather(decays, "seq")
    dz = dot(grads, w_out, MXU_NT).astype(bf16).reshape(2, length, inner)
    state_shape = (2, heads, state, LANES)
    z, dy, adjoint, start = pl.pallas_call(
        partial(outputs_kernel, heads, state, count),
        grid=(2,),
        in_specs=[
            me_spec, by_stream(length, LANES), shared(8, LANES), by_stream(length, inner),
            by_stream(length, inner), shared(1, inner), gathered(count, *state_shape),
            gathered(count, heads, LANES),
        ],
        out_specs=[
            by_stream(length, inner), by_stream(2, length, inner), by_stream(*state_shape),
            by_stream(*state_shape),
        ],
        out_shape=(
            shape_of(bf16, 2, length, inner), shape_of(bf16, 2, 2, length, inner),
            shape_of(bf16, 2, *state_shape), shape_of(f32, 2, *state_shape),
        ),
        scratch_shapes=[pltpu.VMEM((2, length, inner), f32)],
        compiler_params=PARAMS,
    )(me, aux, consts, x, dz, norm_gain[None], all_states, all_decays)
    all_adjoint = lax.all_gather(adjoint, "seq")
    out_terms = dot(z.reshape(2 * length, inner), w_out).reshape(2, length, width)
    out = join_halves(out_terms, parts)
    dx, tail = pl.pallas_call(
        partial(grads_kernel, heads, state, count),
        grid=(2,),
        in_specs=[
            me_spec, by_stream(length, LANES), shared(8, LANES), by_stream(length, inner),
            by_stream(2, length, inner), by_stream(*state_shape), by_stream(*state_shape),
            gathered(count, *state_shape), gathered(count, heads, LANES),
        ],
        out_specs=[by_stream(length, inner), by_stream(length, LANES)],
        out_shape=(shape_of(bf16, 2, length, inner), shape_of(bf16, 2, length, LANES)),
        scratch_shapes=[pltpu.VMEM(state_shape, f32)],
        compiler_params=PARAMS,
    )(me, aux, consts, x, dy, start, states, all_adjoint, all_decays)
    terms = dot(dx.reshape(2 * length, inner), w_value, MXU_NT)
    terms += dot(tail.reshape(2 * length, LANES), w_side, MXU_NT)
    d_hidden = join_halves(terms.reshape(2, length, width), parts)
    return (out, d_hidden)


def solution(mesh):
    in_specs = (
        P("seq", None),
        P("seq"),
        P(None, "mp"),
        P(None, "mp", None),
        P(None, "mp"),
        P("mp"),
        P("mp"),
        P("mp"),
        P("mp"),
        P("mp", None),
        P("seq", None),
    )
    out_specs = (P("seq", "mp"), P("seq", "mp"))
    return jax.shard_map(
        per_device, mesh=mesh, in_specs=in_specs, out_specs=out_specs, check_vma=False
    )
```

profile of v0, /device:TPU:0, one launch (start us, length us, event | category | flops | bytes accessed | tf_op | source)
XLA Modules:
  0.0 204.3 jit_solution(5824129171178994336)
XLA Ops:
  7.2 1.5 copy.18.ids_ref
  8.7 1.2 copy.19
  9.9 1.0 copy.20
  11.0 4.5 %shard_map.122 = (bf16[2,256,2048]{2,1,0:T(8,128)(2,1)}, bf16[2,256,2048]{2,1,0:T(8,128)(2,1)}) custom-call(bf16[256,2048]{1,0:T(8,128)(2,1)} %hidden_ref.1, bf16[256,2048]{1,0:T(8,128)(2,1)} %cot_ref.1, s32[256,1]{1,0:T(8,128)} %copy.18.ids_ref), custom_call_target="tpu_custom_call" | custom-call | tf_op jit(solution)/shard_map/pallas_call | solution.py:307
  15.5 6.3 %convolution_convert_fusion.1 = bf16[512,1024]{1,0:T(8,128)(2,1)} fusion(bf16[512,2048]{1,0:T(8,128)(2,1)} %bitcast.62, bf16[2048,1024]{1,0:T(8,128)(2,1)} %param.13), kind=kOutput, calls=%fused_computation.4 | convolution fusion | flops 2148007936 | bytes 7340032 | tf_op jit(solution)/shard_map/dot_general | solution.py:20
  21.9 1.5 fusion.6.aux_ref
  24.0 3.5 %shard_map.123 = (bf16[2,2,8,32,128]{4,3,2,1,0:T(8,128)(2,1)}, f32[2,8,128]{2,1,0:T(8,128)}) custom-call(f32[2,256,128]{2,1,0:T(8,128)} %fusion.6.aux_ref, f32[8,128]{1,0:T(8,128)} %select_maximum_fusion.consts_ref, bf16[2,256,1024]{2,1,0:T(8,128)(2,1)} %bitcast.45), custom_call_target="tpu_custom_call" | custom-call | tf_op jit(solution)/shard_map/pallas_call | solution.py:321
  27.6 25.6 %all-gather.1 = f32[32,8,128]{2,1,0:T(8,128)} all-gather(f32[2,8,128]{2,1,0:T(8,128)} %get-tuple-element.15), channel_id=3, replica_groups=mesh['seq'=16,'mp'=2] {'seq'}, dimensions={0}, use_global_device_ids=true | all-gather | bytes 139264 | tf_op jit(solution)/shard_map/all_gather | solution.py:330
  53.2 5.6 %convolution_convert_fusion = bf16[512,1024]{1,0:T(8,128)(2,1)} fusion(bf16[512,2048]{1,0:T(8,128)(2,1)S(1)} %bitcast.61, bf16[1024,2048]{1,0:T(8,128)(2,1)} %param.20), kind=kOutput, calls=%fused_computation.3 | convolution fusion | flops 2148007936 | bytes 7340032 | tf_op jit(solution)/shard_map/dot_general | solution.py:20
  58.8 22.3 %all-gather.6.cloned.1.call-done = bf16[32,2,8,32,128]{4,3,2,1,0:T(8,128)(2,1)} async-done(((bf16[2,2,8,32,128]{4,3,2,1,0:T(8,128)(2,1)}), bf16[32,2,8,32,128]{4,3,2,1,0:T(8,128)(2,1)}) %all-gather.6.cloned.1.call-update) | async-done | bytes 4194320 | tf_op jit(solution)/shard_map/all_gather | solution.py:329
  81.1 16.6 %shard_map.124 = (bf16[2,256,1024]{2,1,0:T(8,128)(2,1)}, bf16[2,2,256,1024]{3,2,1,0:T(8,128)(2,1)}, bf16[2,2,8,32,128]{4,3,2,1,0:T(8,128)(2,1)}, f32[2,2,8,32,128]{4,3,2,1,0:T(8,128)}) custom-call(s32[1]{0:T(128)} %bitcast.me_ref, f32[2,256,128]{2,1,0:T(8,128)} %fusion.6.aux_ref, f32[8,128]{1,0:T(8,128)} %select_maximum_fusion.consts_ref, ...), custom_call_target="tpu_custom_call" | custom-call | tf_op jit(solution)/shard_map/pallas_call | solution.py:333
  97.8 6.8 %fusion.terms_ref = f32[2,256,2048]{2,1,0:T(8,128)} fusion(bf16[2,256,1024]{2,1,0:T(8,128)(2,1)} %get-tuple-element.16, bf16[1024,2048]{1,0:T(8,128)(2,1)} %param.20), kind=kOutput, calls=%fused_computation | convolution fusion | flops 2147483648 | bytes 9437184 | tf_op jit(solution)/shard_map/dot_general | solution.py:20
  104.6 4.0 %shard_map.125 = f32[2,256,1024]{2,1,0:T(8,128)} custom-call(f32[2,256,2048]{2,1,0:T(8,128)} %fusion.terms_ref), custom_call_target="tpu_custom_call" | custom-call | tf_op jit(solution)/shard_map/pallas_call | solution.py:280
  108.6 2.1 %fusion.4 = bf16[256,1024]{1,0:T(8,128)(2,1)} fusion(f32[2,256,1024]{2,1,0:T(8,128)} %shard_map.125, s32[]{:T(128)S(6)} %select_n.10), kind=kLoop, calls=%fused_computation.11 | loop fusion | bytes 1048580 | tf_op jit(solution)/shard_map/convert_element_type | solution.py:289
  110.7 1.5 collective-permute-start
  112.3 34.5 %all-gather.8.cloned.1.call-done = bf16[32,2,8,32,128]{4,3,2,1,0:T(8,128)(2,1)} async-done(((bf16[2,2,8,32,128]{4,3,2,1,0:T(8,128)(2,1)}), bf16[32,2,8,32,128]{4,3,2,1,0:T(8,128)(2,1)}) %all-gather.8.cloned.1.call-update) | async-done | bytes 4194320 | tf_op jit(solution)/shard_map/all_gather | solution.py:352
  146.8 21.6 %shard_map.126 = (bf16[2,256,1024]{2,1,0:T(8,128)(2,1)}, bf16[2,256,128]{2,1,0:T(8,128)(2,1)}) custom-call(s32[1]{0:T(128)} %bitcast.me_ref, f32[2,256,128]{2,1,0:T(8,128)} %fusion.6.aux_ref, f32[8,128]{1,0:T(8,128)} %select_maximum_fusion.consts_ref, bf16[2,256,1024]{2,1,0:T(8,128)(2,1)} %bitcast.47, bf16[2,2,256,1024]{3,2,1,0:T(8,128)(2,1)} %get-tuple-element.17.dy_ref, ...), custom_call_target="tpu_custom_call" | custom-call | tf_op jit(solution)/shard_map/pallas_call | solution.py:355
  168.3 3.6 %fusion.10 = f32[512,2048]{1,0:T(8,128)S(1)} fusion(bf16[512,1024]{1,0:T(8,128)(2,1)} %bitcast.63, bf16[2048,1024]{1,0:T(8,128)(2,1)S(1)} %copy-done.5), kind=kOutput, calls=%fused_computation.22 | convolution fusion | flops 2147483648 | bytes 9437184 | tf_op jit(solution)/shard_map/dot_general | solution.py:20
  172.0 2.8 %convolution_add_fusion = f32[512,2048]{1,0:T(8,128)} fusion(f32[512,2048]{1,0:T(8,128)S(1)} %fusion.10, bf16[512,128]{1,0:T(8,128)(2,1)S(1)} %bitcast.55, bf16[2048,64]{1,0:T(8,128)(2,1)S(1)} %bitcast.51, bf16[2048,8]{1,0:T(8,128)(2,1)S(1)} %copy.20, bf16[128]{0:T(256)(128)(2,1)S(1)} %pad.9.clone), kind=kOutput, calls=%fused_computation.2 | convolution fusion | flops 271056896 | bytes 8814848 | tf_op jit(solution)/shard_map/dot_general | solution.py:20
  174.7 4.1 %shard_map.127 = f32[2,256,1024]{2,1,0:T(8,128)} custom-call(f32[2,256,2048]{2,1,0:T(8,128)} %bitcast.44), custom_call_target="tpu_custom_call" | custom-call | tf_op jit(solution)/shard_map/pallas_call | solution.py:280
  178.9 2.1 %fusion.5 = bf16[256,1024]{1,0:T(8,128)(2,1)} fusion(f32[2,256,1024]{2,1,0:T(8,128)} %shard_map.127, s32[]{:T(128)S(6)} %select_n.10), kind=kLoop, calls=%fused_computation.12 | loop fusion | bytes 1048580 | tf_op jit(solution)/shard_map/convert_element_type | solution.py:289
  181.0 1.5 collective-permute-start.1
  183.4 11.9 %collective-permute-done.1 = bf16[256,1024]{1,0:T(8,128)(2,1)S(1)} collective-permute-done((bf16[256,1024]{1,0:T(8,128)(2,1)}, bf16[256,1024]{1,0:T(8,128)(2,1)S(1)}, u32[]{:S(2)}, u32[]{:S(2)}) %collective-permute-start.1) | collective-permute-done | bytes 524320 | tf_op jit(solution)/shard_map/ppermute | solution.py:290
  195.3 2.2 %fusion.2 = bf16[256,1024]{1,0:T(8,128)(2,1)} fusion(bf16[256,1024]{1,0:T(8,128)(2,1)S(1)} %collective-permute-done.1, f32[2,256,1024]{2,1,0:T(8,128)} %shard_map.127, s32[]{:T(128)S(6)} %select_n.9), kind=kLoop, calls=%fused_computation.6 | loop fusion | flops 786432 | bytes 2097156 | tf_op jit(solution)/shard_map/convert_element_type | solution.py:293
  (25 shorter events, 1.8 us)
Async XLA Ops:
  7.2 73.9 %all-gather.6.cloned.1.call-start = ((), (), s32[]{:S(2)}) async-start(), calls=%async_computation | async-start | bytes 4456448 | tf_op jit(solution)/shard_map/all_gather | solution.py:329
  15.5 6.3 %copy-start.7 = (bf16[2,256,2048]{2,1,0:T(8,128)(2,1)S(1)}, bf16[2,256,2048]{2,1,0:T(8,128)(2,1)}, u32[]{:S(2)}) copy-start(bf16[2,256,2048]{2,1,0:T(8,128)(2,1)} %get-tuple-element.12) | copy-start | bytes 6291460
  15.5 7.8 %copy-start.2 = (f32[8]{0:T(128)S(1)}, f32[8]{0:T(128)}, u32[]{:S(2)}) copy-start(f32[8]{0:T(128)} %param.18) | copy-start | bytes 100
  15.5 7.8 %copy-start.3 = (f32[8]{0:T(128)S(1)}, f32[8]{0:T(128)}, u32[]{:S(2)}) copy-start(f32[8]{0:T(128)} %param.17) | copy-start | bytes 100
  15.5 7.8 %copy-start.4 = (f32[8]{0:T(128)S(1)}, f32[8]{0:T(128)}, u32[]{:S(2)}) copy-start(f32[8]{0:T(128)} %param.16) | copy-start | bytes 100
  21.9 31.3 %copy-start.6 = (bf16[2,256,2048]{2,1,0:T(8,128)(2,1)S(1)}, bf16[2,256,2048]{2,1,0:T(8,128)(2,1)}, u32[]{:S(2)}) copy-start(bf16[2,256,2048]{2,1,0:T(8,128)(2,1)} %get-tuple-element.13) | copy-start | bytes 6291460
  27.5 119.2 %all-gather.8.cloned.1.call-start = ((), (), s32[]{:S(2)}) async-start(), calls=%async_computation.1 | async-start | bytes 4456448 | tf_op jit(solution)/shard_map/all_gather | solution.py:352
  110.7 71.7 %collective-permute-start = (bf16[256,1024]{1,0:T(8,128)(2,1)}, bf16[256,1024]{1,0:T(8,128)(2,1)S(1)}, u32[]{:S(2)}, u32[]{:S(2)}) collective-permute-start(bf16[256,1024]{1,0:T(8,128)(2,1)} %fusion.4), channel_id=1, source_target_pairs={{0,1},{1,0},{2,3},{3,2},{4,5},{5,4},{6,7},{7,6},{8,9},{9,8},{10,11... | collective-permute-start | bytes 1572872 | tf_op jit(solution)/shard_map/ppermute | solution.py:290
  146.8 21.6 %copy-start.5 = (bf16[2048,1024]{1,0:T(8,128)(2,1)S(1)}, bf16[2048,1024]{1,0:T(8,128)(2,1)}, u32[]{:S(2)}) copy-start(bf16[2048,1024]{1,0:T(8,128)(2,1)} %param.13) | copy-start | bytes 12582916
  168.3 3.6 %copy-start.1 = (bf16[2,256,128]{2,1,0:T(8,128)(2,1)S(1)}, bf16[2,256,128]{2,1,0:T(8,128)(2,1)}, u32[]{:S(2)}) copy-start(bf16[2,256,128]{2,1,0:T(8,128)(2,1)} %get-tuple-element.21) | copy-start | bytes 393220
  174.7 7.7 %copy-start = (f32[2,256,1024]{2,1,0:T(8,128)S(1)}, f32[2,256,1024]{2,1,0:T(8,128)}, u32[]{:S(2)}) copy-start(f32[2,256,1024]{2,1,0:T(8,128)} %shard_map.125) | copy-start | bytes 6291460
  181.0 14.3 %collective-permute-start.1 = (bf16[256,1024]{1,0:T(8,128)(2,1)}, bf16[256,1024]{1,0:T(8,128)(2,1)S(1)}, u32[]{:S(2)}, u32[]{:S(2)}) collective-permute-start(bf16[256,1024]{1,0:T(8,128)(2,1)} %fusion.5), channel_id=1, source_target_pairs={{0,1},{1,0},{2,3},{3,2},{4,5},{5,4},{6,7},{7,6},{8,9},{9,8},{10,11... | collective-permute-start | bytes 1572872 | tf_op jit(solution)/shard_map/ppermute | solution.py:290
Sparse Core Ops, SparseCore 0:
  27.6 53.4 all-gather.5
  97.9 48.8 all-gather.7
where the time goes:
time: 205 us; the launch traced here: 204 us
  waiting for transfers between devices  68.7 us (34%)
  Pallas kernels  54.4 us (27%)
  matrix products  26.7 us (13%)
  blocking collectives  25.6 us (12%)
  between operations  14.1 us (7%)
  local copies, waits for them, and re-layouts  8.02 us (4%)
  other arithmetic  3.69 us (2%)
  starting transfers between devices  3.07 us (1%)
    all_gather x1, waiting for transfers between devices, per_device(): all_adjoint = lax.all_gather(adjoint, 'seq')  34.5 us
    dot_general x6, matrix products, dot(): lax.dot_general(a, b, dims, preferred_element_type=f32, precision=precision)  26.7 us
    all_gather x1, blocking collectives, per_device(): all_decays = lax.all_gather(decays, 'seq')  25.6 us
    all_gather x1, waiting for transfers between devices, per_device(): all_states = lax.all_gather(states, 'seq')  22.3 us
    pallas_call x1, Pallas kernels, per_device(): pl.pallas_call(partial(grads_kernel, heads, state, count), grid=(2,), in_...  21.6 us
    pallas_call x1, Pallas kernels, per_device(): pl.pallas_call(partial(outputs_kernel, heads, state, count), grid=(2,), i...  16.6 us
    ppermute x2, waiting for transfers between devices, join_halves(): lax.ppermute(leaving, 'mp', [(i, (i + hop) % parts) for i in range(parts)])  11.9 us
    pallas_call x2, Pallas kernels, join_halves(): pl.pallas_call(merge_kernel, out_shape=shape_of(f32, parts, length, width...  8.16 us
  transfers between devices with their start and end apart: 4, of which 3 were waited for; matrix products, arithmetic and copies ran while one was open for 12% of the time, Pallas kernels for 15%

commit v1 on v0

--- a/solution.py
+++ b/solution.py
@@ -65,7 +65,120 @@
     return shifted, dt, la, cum, cum - la
 
 
-def ends_kernel(heads, state, aux_ref, consts_ref, x_ref, st_ref, dec_ref):
+def put_rows(parcel_ref, h, which, value):
+    count, _, _, rows, _ = parcel_ref.shape
+    per = value.shape[0] // rows
+    for k in range(per):
+        parcel_ref[h * per + k, 0, which] = value[k * rows : (k + 1) * rows].astype(bf16)
+
+
+def put_decay(parcel_ref, h, heads, decay):
+    count, _, _, rows, _ = parcel_ref.shape
+    per = count // heads
+    wide = jnp.broadcast_to(decay, (rows, LANES))
+    main = wide.astype(bf16)
+    rest = (wide - main.astype(f32)).astype(bf16)
+    for k in range(per):
+        parcel_ref[h * per + k, 0, 2] = main
+        parcel_ref[h * per + k, 0, 3] = rest
+
+
+def take_rows(parcel_ref, h, heads, which):
+    per = parcel_ref.shape[0] // heads
+    pieces = [parcel_ref[h * per + k, 0, which].astype(f32) for k in range(per)]
+    return jnp.concatenate(pieces, axis=0)
+
+
+def exchange_kernel(
+    upward, parcel_ref, out_ref, got, back, final, send_out, recv_out, send_back, recv_back
+):
+    count = parcel_ref.shape[0]
+    me = lax.axis_index("seq")
+    barrier = pltpu.get_barrier_semaphore()
+    mesh_id = pl.DeviceIdType.MESH
+
+    def peer_of(hop):
+        return lax.rem(me + hop, count)
+
+    def greet(hop, none):
+        pl.semaphore_signal(
+            barrier, inc=1, device_id={"seq": peer_of(hop)}, device_id_type=mesh_id
+        )
+        return none
+
+    lax.fori_loop(1, count, greet, 0)
+    pl.semaphore_wait(barrier, count - 1)
+
+    def outward(hop):
+        return pltpu.make_async_remote_copy(
+            src_ref=parcel_ref.at[peer_of(hop)], dst_ref=got.at[me],
+            send_sem=send_out.at[hop], recv_sem=recv_out.at[hop],
+            device_id={"seq": peer_of(hop)}, device_id_type=mesh_id,
+        )
+
+    def homeward(hop):
+        return pltpu.make_async_remote_copy(
+            src_ref=back.at[peer_of(hop)], dst_ref=final.at[me],
+            send_sem=send_back.at[hop], recv_sem=recv_back.at[hop],
+            device_id={"seq": peer_of(hop)}, device_id_type=mesh_id,
+        )
+
+    def start(copy):
+        def step(hop, none):
+            copy(hop).start()
+            return none
+
+        lax.fori_loop(1, count, step, 0)
+
+    def finish(copy):
+        def step(hop, none):
+            copy(hop).wait()
+            return none
+
+        lax.fori_loop(1, count, step, 0)
+
+    start(outward)
+    got[me] = parcel_ref[me]
+    finish(outward)
+    rows = got.shape[3]
+    zero = jnp.zeros((2, rows, LANES), f32)
+
+    def scan(i, totals):
+        result = []
+        for which in range(2):
+            j = count - 1 - i if (which == 1) != upward else i
+            total = totals[which]
+            back[j, :, which] = total.astype(bf16)
+            decay = got[j, :, 2].astype(f32) + got[j, :, 3].astype(f32)
+            result.append(decay * total + got[j, :, which].astype(f32))
+        return tuple(result)
+
+    lax.fori_loop(0, count, scan, (zero, zero))
+    start(homeward)
+    final[me] = back[me]
+    finish(homeward)
+    out_ref[...] = final[...]
+
+
+def exchange(parcels, upward, collective_id):
+    count, streams, _, rows, _ = parcels.shape
+    carried = (count, streams, 2, rows, LANES)
+    return pl.pallas_call(
+        partial(exchange_kernel, upward),
+        in_specs=[pl.BlockSpec(memory_space=pltpu.VMEM)],
+        out_specs=pl.BlockSpec(memory_space=pltpu.VMEM),
+        out_shape=shape_of(bf16, *carried),
+        scratch_shapes=[
+            pltpu.VMEM(parcels.shape, bf16), pltpu.VMEM(carried, bf16), pltpu.VMEM(carried, bf16),
+        ] + [pltpu.SemaphoreType.DMA((count,))] * 4,
+        compiler_params=pltpu.CompilerParams(
+            collective_id=collective_id, has_side_effects=True,
+            vmem_limit_bytes=32 * 1024 * 1024,
+        ),
+    )(parcels)
+
+
+def ends_kernel(heads, state, aux_ref, consts_ref, x_ref, st_ref):
     aux = aux_ref[0]
     length = aux.shape[0]
     _, dt, la, cum, exc = prepare(aux, consts_ref[...])
@@ -76,31 +189,19 @@
     w_r = jnp.exp(exc_t) * dt_t
     for h in range(heads):
         left = jnp.concatenate([b_t * w_f[h : h + 1], b_t * w_r[h : h + 1]], axis=0).astype(bf16)
-        both = dot(left, x_ref[0, :, pl.ds(h * LANES, LANES)]).astype(bf16)
-        st_ref[0, 0, h] = both[:state]
-        st_ref[0, 1, h] = both[state:]
-    dec_ref[0] = jnp.broadcast_to(end, (heads, LANES))
-
-
-def carried(me, count, all_ref, dec_ref, which, upward):
-    shape = all_ref.shape[3:]
-
-    def step(i, total):
-        j = (count - 1 - i) if upward else i
-        return jnp.exp(dec_ref[j, 0])[:, None, :] * total + all_ref[j, 0, which].astype(f32)
-
-    steps = (count - 1 - me) if upward else me
-    return lax.fori_loop(0, steps, step, jnp.zeros(shape, f32))
+        both = dot(left, x_ref[0, :, pl.ds(h * LANES, LANES)])
+        put_rows(st_ref, h, 0, both[:state])
+        put_rows(st_ref, h, 1, both[state:])
+        put_decay(st_ref, h, heads, jnp.exp(end[h : h + 1]))
 
 
 def outputs_kernel(
-    heads, state, count,
-    me_ref, aux_ref, consts_ref, x_ref, dz_ref, gain_ref, st_ref, dec_ref,
-    z_ref, dy_ref, adj_ref, start_ref, y_scr,
+    heads, state,
+    aux_ref, consts_ref, x_ref, dz_ref, gain_ref, start_ref,
+    z_ref, dy_ref, adj_ref, y_scr,
 ):
     aux, consts = aux_ref[0], consts_ref[...]
     length = aux.shape[0]
-    me = me_ref[0]
     _, dt, la, cum, exc = prepare(aux, consts)
     cum_t, exc_t, dt_t = cum.T[:heads], exc.T[:heads], dt.T[:heads]
     end_t = cum_t[:, length - 1 : length]
@@ -109,8 +210,6 @@
     c_m = rounded[:, LANES - state :]
     c32 = c_m.astype(f32)
     c_t = rounded.astype(f32).T[LANES - state :]
-    start_ref[0, 0] = carried(me, count, st_ref, dec_ref, 0, False)
-    start_ref[0, 1] = carried(me, count, st_ref, dec_ref, 1, True)
     scores = dot(c_m, b_m, MXU_NT)
     rows, cols = iota2((length, length), 0), iota2((length, length), 1)
     grow_f = jnp.exp(cum)
@@ -129,9 +228,9 @@
         x_h = x_ref[0, :, at]
         direct = consts[2:3, one] * x_h.astype(f32)
         y_f = dot(low, x_h) + direct
-        y_f += dot((c32 * grow_f[:, one]).astype(bf16), start_ref[0, 0, h].astype(bf16))
+        y_f += dot((c32 * grow_f[:, one]).astype(bf16), take_rows(start_ref, h, heads, 0).astype(bf16))
         y_r = dot(high, x_h) + direct
-        y_r += dot((c32 * grow_r[:, one]).astype(bf16), start_ref[0, 1, h].astype(bf16))
+        y_r += dot((c32 * grow_r[:, one]).astype(bf16), take_rows(start_ref, h, heads, 1).astype(bf16))
         y_scr[0, :, at] = y_f
         y_scr[1, :, at] = y_r
         sq_f += jnp.sum(y_f * y_f, axis=1, keepdims=True)
@@ -160,18 +259,18 @@
         d_r = (rs_r * (g - y_scr[1, :, at] * rs_r * m_r)).astype(bf16)
         dy_ref[0, 0, :, at] = d_f
         dy_ref[0, 1, :, at] = d_r
-        adj_ref[0, 0, h] = dot((c_t * out_f[one]).astype(bf16), d_f).astype(bf16)
-        adj_ref[0, 1, h] = dot((c_t * out_r[one]).astype(bf16), d_r).astype(bf16)
+        put_rows(adj_ref, h, 0, dot((c_t * out_f[one]).astype(bf16), d_f))
+        put_rows(adj_ref, h, 1, dot((c_t * out_r[one]).astype(bf16), d_r))
+        put_decay(adj_ref, h, heads, jnp.exp(end_t[one]))
 
 
 def grads_kernel(
-    heads, state, count,
-    me_ref, aux_ref, consts_ref, x_ref, dy_ref, start_ref, own_ref, adj_ref, dec_ref,
-    dx_ref, tail_ref, in_scr,
+    heads, state,
+    aux_ref, consts_ref, x_ref, dy_ref, start_ref, own_ref, in_ref,
+    dx_ref, tail_ref,
 ):
     aux, consts = aux_ref[0], consts_ref[...]
     length = aux.shape[0]
-    me = me_ref[0]
     shifted, dt, la, cum, exc = prepare(aux, consts)
     cum_t, exc_t = cum.T[:heads], exc.T[:heads]
     end = cum[length - 1 : length]
@@ -179,8 +278,6 @@
     b_m = rounded[:, LANES - 2 * state : LANES - state]
     c_m = rounded[:, LANES - state :]
     b32, c32 = b_m.astype(f32), c_m.astype(f32)
-    in_scr[0] = carried(me, count, adj_ref, dec_ref, 0, True)
-    in_scr[1] = carried(me, count, adj_ref, dec_ref, 1, False)
     scores_t = dot(b_m, c_m, MXU_NT)
     rows, cols = iota2((length, length), 0), iota2((length, length), 1)
     lane = iota2((length, LANES), 1)
@@ -200,8 +297,8 @@
         at = pl.ds(h * LANES, LANES)
         one = slice(h, h + 1)
         x_h, d_f, d_r = x_ref[0, :, at], dy_ref[0, 0, :, at], dy_ref[0, 1, :, at]
-        s_f, s_r = start_ref[0, 0, h], start_ref[0, 1, h]
-        a_f, a_r = in_scr[0, h], in_scr[1, h]
+        s_f, s_r = take_rows(start_ref, h, heads, 0), take_rows(start_ref, h, heads, 1)
+        a_f, a_r = take_rows(in_ref, h, heads, 0), take_rows(in_ref, h, heads, 1)
         dt_h = dt[:, one]
         decay = jnp.exp(
             jnp.where(cols >= rows, cum_t[one] - cum[:, one], exc[:, one] - exc_t[one])
@@ -237,7 +334,7 @@
         into_r = jnp.where(lane == h, in_r, into_r)
         carry_f = jnp.where(lane == h, c_f, carry_f)
         carry_r = jnp.where(lane == h, c_r, carry_r)
-        ending = a_f * (end_decay[:, one] * s_f + own_ref[0, 0, h].astype(f32))
+        ending = a_f * (end_decay[:, one] * s_f + take_rows(own_ref, h, heads, 0))
         ending += a_r * (end_decay[:, one] * s_r)
         ended = jnp.sum(jnp.sum(ending, axis=1, keepdims=True), axis=0, keepdims=True)
         ended += jnp.sum(c_r, axis=0, keepdims=True)
@@ -302,8 +399,6 @@
     state = w_bc.shape[2] // 2
     assert w_bc.shape[1] == 1 and inner == heads * LANES
     count, parts = lax.axis_size("seq"), lax.axis_size("mp")
-    me = lax.axis_index("seq").reshape(1).astype(jnp.int32)
-    me_spec = pl.BlockSpec(memory_space=pltpu.SMEM)
     sources, grads = pl.pallas_call(
         sources_kernel,
         out_shape=(shape_of(bf16, 2, length, width),) * 2,
@@ -318,53 +413,52 @@
     )
     aux = dot(sources, w_side).reshape(2, length, LANES)
     x = dot(sources, w_value).astype(bf16).reshape(2, length, inner)
-    states, decays = pl.pallas_call(
+    assert count % heads == 0 and (heads * state) % count == 0
+    rows = heads * state // count
+    parcel = (count, 2, 4, rows, LANES)
+    states = pl.pallas_call(
         partial(ends_kernel, heads, state),
         grid=(2,),
         in_specs=[by_stream(length, LANES), shared(8, LANES), by_stream(length, inner)],
-        out_specs=[by_stream(2, heads, state, LANES), by_stream(heads, LANES)],
-        out_shape=(shape_of(bf16, 2, 2, heads, state, LANES), shape_of(f32, 2, heads, LANES)),
+        out_specs=gathered(count, 4, rows, LANES),
+        out_shape=shape_of(bf16, *parcel),
         compiler_params=PARAMS,
     )(aux, consts, x)
-    all_states = lax.all_gather(states, "seq")
-    all_decays = lax.all_gather(decays, "seq")
+    starts = exchange(states, False, 0)
     dz = dot(grads, w_out, MXU_NT).astype(bf16).reshape(2, length, inner)
-    state_shape = (2, heads, state, LANES)
-    z, dy, adjoint, start = pl.pallas_call(
-        partial(outputs_kernel, heads, state, count),
+    z, dy, adjoint = pl.pallas_call(
+        partial(outputs_kernel, heads, state),
         grid=(2,),
         in_specs=[
-            me_spec, by_stream(length, LANES), shared(8, LANES), by_stream(length, inner),
-            by_stream(length, inner), shared(1, inner), gathered(count, *state_shape),
-            gathered(count, heads, LANES),
+            by_stream(length, LANES), shared(8, LANES), by_stream(length, inner),
+            by_stream(length, inner), shared(1, inner), gathered(count, 2, rows, LANES),
         ],
         out_specs=[
-            by_stream(length, inner), by_stream(2, length, inner), by_stream(*state_shape),
-            by_stream(*state_shape),
+            by_stream(length, inner), by_stream(2, length, inner),
+            gathered(count, 4, rows, LANES),
         ],
         out_shape=(
             shape_of(bf16, 2, length, inner), shape_of(bf16, 2, 2, length, inner),
-            shape_of(bf16, 2, *state_shape), shape_of(f32, 2, *state_shape),
+            shape_of(bf16, *parcel),
         ),
         scratch_shapes=[pltpu.VMEM((2, length, inner), f32)],
         compiler_params=PARAMS,
-    )(me, aux, consts, x, dz, norm_gain[None], all_states, all_decays)
-    all_adjoint = lax.all_gather(adjoint, "seq")
+    )(aux, consts, x, dz, norm_gain[None], starts)
     out_terms = dot(z.reshape(2 * length, inner), w_out).reshape(2, length, width)
     out = join_halves(out_terms, parts)
+    arriving = exchange(adjoint, True, 1)
     dx, tail = pl.pallas_call(
-        partial(grads_kernel, heads, state, count),
+        partial(grads_kernel, heads, state),
         grid=(2,),
         in_specs=[
-            me_spec, by_stream(length, LANES), shared(8, LANES), by_stream(length, inner),
-            by_stream(2, length, inner), by_stream(*state_shape), by_stream(*state_shape),
-            gathered(count, *state_shape), gathered(count, heads, LANES),
+            by_stream(length, LANES), shared(8, LANES), by_stream(length, inner),
+            by_stream(2, length, inner), gathered(count, 2, rows, LANES),
+            gathered(count, 4, rows, LANES), gathered(count, 2, rows, LANES),
         ],
         out_specs=[by_stream(length, inner), by_stream(length, LANES)],
         out_shape=(shape_of(bf16, 2, length, inner), shape_of(bf16, 2, length, LANES)),
-        scratch_shapes=[pltpu.VMEM(state_shape, f32)],
         compiler_params=PARAMS,
-    )(me, aux, consts, x, dy, start, states, all_adjoint, all_decays)
+    )(aux, consts, x, dy, starts, states, arriving)
     terms = dot(dx.reshape(2 * length, inner), w_value, MXU_NT)
     terms += dot(tail.reshape(2 * length, LANES), w_side, MXU_NT)
     d_hidden = join_halves(terms.reshape(2, length, width), parts)

time: 205 us -> 158 us (0.77)
  waiting for transfers between devices: 68.7 us -> 12.4 us
  Pallas kernels: 54.4 us -> 100 us
  blocking collectives: 25.6 us -> 0 us
  between operations: 14.1 us -> 0.74 us
  local copies, waits for them, and re-layouts: 8.02 us -> 10.8 us
    all_gather x2 -> x0, waiting for transfers between devices: 56.8 us -> none  [the longest x1 34.5 us: per_device(): all_adjoint = lax.all_gather(adjoint, 'seq')]
    pallas_call x2 -> x4, Pallas kernels: 38.2 us -> 83.9 us  [the longest x2 49.9 us: exchange(): pl.pallas_call(partial(exchange_kernel, upward), in_specs=[pl.BlockSpec(m...]
    all_gather x1 -> x0, blocking collectives: 25.6 us -> none  [per_device(): all_decays = lax.all_gather(decays, 'seq')]
    unnamed x18 -> x26, local copies, waits for them, and re-layouts: 2.28 us -> 5.06 us
  transfers between devices with their start and end apart: 4 -> 2, of which waited for: 3 -> 1; matrix products, arithmetic and copies ran while one was open for 12% -> 6% of each run, Pallas kernels for 15% -> 3%
where the time goes in v1:
time: 158 us
  Pallas kernels  100 us (63%)
  matrix products  27.8 us (18%)
  waiting for transfers between devices  12.4 us (8%)
  local copies, waits for them, and re-layouts  10.8 us (7%)
  other arithmetic  3.71 us (2%)
  starting transfers between devices  2.03 us (1%)
    pallas_call x2, Pallas kernels, exchange(): pl.pallas_call(partial(exchange_kernel, upward), in_specs=[pl.BlockSpec(m...  49.9 us
    dot_general x6, matrix products, dot(): lax.dot_general(a, b, dims, preferred_element_type=f32, precision=precision)  27.8 us
    pallas_call x1, Pallas kernels, per_device(): pl.pallas_call(partial(grads_kernel, heads, state), grid=(2,), in_specs=[...  19.4 us
    pallas_call x1, Pallas kernels, per_device(): pl.pallas_call(partial(outputs_kernel, heads, state), grid=(2,), in_specs...  14.6 us
    ppermute x2, waiting for transfers between devices, join_halves(): lax.ppermute(leaving, 'mp', [(i, (i + hop) % parts) for i in range(parts)])  12.4 us
    pallas_call x2, Pallas kernels, join_halves(): pl.pallas_call(merge_kernel, out_shape=shape_of(f32, parts, length, width...  8.17 us
    unnamed x26, local copies, waits for them, and re-layouts  5.06 us
    pallas_call x1, Pallas kernels, per_device(): pl.pallas_call(sources_kernel, out_shape=(shape_of(bf16, 2, length, width...  4.46 us
  transfers between devices with their start and end apart: 2, of which 1 were waited for; matrix products, arithmetic and copies ran while one was open for 6% of the time, Pallas kernels for 3%

profile of v1, /device:TPU:0, one launch (start us, length us, event | category | flops | bytes accessed | tf_op | source)
XLA Modules:
  0.0 157.6 jit_solution(4035258066556238038)
XLA Ops:
  0.6 1.5 copy.15.ids_ref
  2.1 1.2 copy.16
  3.3 1.0 copy.17
  4.5 4.5 %shard_map.122 = (bf16[2,256,2048]{2,1,0:T(8,128)(2,1)}, bf16[2,256,2048]{2,1,0:T(8,128)(2,1)}) custom-call(bf16[256,2048]{1,0:T(8,128)(2,1)} %hidden_ref.1, bf16[256,2048]{1,0:T(8,128)(2,1)} %cot_ref.1, s32[256,1]{1,0:T(8,128)} %copy.15.ids_ref), custom_call_target="tpu_custom_call" | custom-call | tf_op jit(solution)/shard_map/pallas_call | solution.py:402
  8.9 6.3 %convolution_convert_fusion.1 = bf16[512,1024]{1,0:T(8,128)(2,1)} fusion(bf16[512,2048]{1,0:T(8,128)(2,1)} %bitcast.54, bf16[2048,1024]{1,0:T(8,128)(2,1)} %param.13), kind=kOutput, calls=%fused_computation.4 | convolution fusion | flops 2148007936 | bytes 7340032 | tf_op jit(solution)/shard_map/dot_general | solution.py:20
  15.2 1.5 fusion.6.aux_ref
  17.4 3.6 %shard_map.123.parcel_ref.own_ref = bf16[16,2,4,16,128]{4,3,2,1,0:T(8,128)(2,1)} custom-call(f32[2,256,128]{2,1,0:T(8,128)} %fusion.6.aux_ref, f32[8,128]{1,0:T(8,128)} %select_maximum_fusion.consts_ref, bf16[2,256,1024]{2,1,0:T(8,128)(2,1)} %bitcast.41), custom_call_target="tpu_custom_call" | custom-call | tf_op jit(solution)/shard_map/pallas_call | solution.py:419
  20.9 1.0 copy-done
  22.0 27.4 %shard_map.124.start_ref = bf16[16,2,2,16,128]{4,3,2,1,0:T(8,128)(2,1)S(1)} custom-call(bf16[16,2,4,16,128]{4,3,2,1,0:T(8,128)(2,1)S(1)} %copy-done), custom_call_target="tpu_custom_call" | custom-call | tf_op jit(solution)/shard_map/pallas_call | solution.py:166
  49.4 5.8 %convolution_convert_fusion = bf16[512,1024]{1,0:T(8,128)(2,1)} fusion(bf16[512,2048]{1,0:T(8,128)(2,1)S(1)} %bitcast.53, bf16[1024,2048]{1,0:T(8,128)(2,1)} %param.20), kind=kOutput, calls=%fused_computation.3 | convolution fusion | flops 2148007936 | bytes 7340032 | tf_op jit(solution)/shard_map/dot_general | solution.py:20
  55.2 14.6 %shard_map.125 = (bf16[2,256,1024]{2,1,0:T(8,128)(2,1)}, bf16[2,2,256,1024]{3,2,1,0:T(8,128)(2,1)}, bf16[16,2,4,16,128]{4,3,2,1,0:T(8,128)(2,1)}) custom-call(f32[2,256,128]{2,1,0:T(8,128)} %fusion.6.aux_ref, f32[8,128]{1,0:T(8,128)} %select_maximum_fusion.consts_ref, bf16[2,256,1024]{2,1,0:T(8,128)(2,1)} %bitcast.42, bf16[2,256,1024]{2,1,0:T(8,128)(2,1)} %bitcast.46, ...), custom_call_target="tpu_custom_call" | custom-call | tf_op jit(solution)/shard_map/pallas_call | solution.py:429
  69.8 1.0 copy-done.3
  70.9 22.5 %shard_map.127.in_ref = bf16[16,2,2,16,128]{4,3,2,1,0:T(8,128)(2,1)S(1)} custom-call(bf16[16,2,4,16,128]{4,3,2,1,0:T(8,128)(2,1)S(1)} %copy-done.3), custom_call_target="tpu_custom_call" | custom-call | tf_op jit(solution)/shard_map/pallas_call | solution.py:166
  94.1 19.4 %shard_map.128 = (bf16[2,256,1024]{2,1,0:T(8,128)(2,1)}, bf16[2,256,128]{2,1,0:T(8,128)(2,1)}) custom-call(f32[2,256,128]{2,1,0:T(8,128)} %fusion.6.aux_ref, f32[8,128]{1,0:T(8,128)} %select_maximum_fusion.consts_ref, bf16[2,256,1024]{2,1,0:T(8,128)(2,1)} %bitcast.43, bf16[2,2,256,1024]{3,2,1,0:T(8,128)(2,1)} %get-tuple-element.12.dy_ref, ...), custom_call_target="tpu_custom_call" | custom-call | tf_op jit(solution)/shard_map/pallas_call | solution.py:450
  113.4 4.9 %fusion.10 = f32[512,2048]{1,0:T(8,128)S(1)} fusion(bf16[512,1024]{1,0:T(8,128)(2,1)} %bitcast.55, bf16[2048,1024]{1,0:T(8,128)(2,1)} %param.13), kind=kOutput, calls=%fused_computation.22 | convolution fusion | flops 2147483648 | bytes 9437184 | tf_op jit(solution)/shard_map/dot_general | solution.py:20
  118.4 2.8 %convolution_add_fusion = f32[512,2048]{1,0:T(8,128)} fusion(f32[512,2048]{1,0:T(8,128)S(1)} %fusion.10, bf16[512,128]{1,0:T(8,128)(2,1)S(1)} %bitcast.47, bf16[2048,64]{1,0:T(8,128)(2,1)S(1)} %bitcast.45, bf16[2048,8]{1,0:T(8,128)(2,1)S(1)} %copy.17, bf16[128]{0:T(256)(128)(2,1)S(1)} %pad.9.clone), kind=kOutput, calls=%fused_computation.2 | convolution fusion | flops 271056896 | bytes 8814848 | tf_op jit(solution)/shard_map/dot_general | solution.py:20
  121.2 4.1 %shard_map.129 = f32[2,256,1024]{2,1,0:T(8,128)} custom-call(f32[2,256,2048]{2,1,0:T(8,128)} %bitcast.40), custom_call_target="tpu_custom_call" | custom-call | tf_op jit(solution)/shard_map/pallas_call | solution.py:377
  125.2 2.1 %fusion.5 = bf16[256,1024]{1,0:T(8,128)(2,1)} fusion(f32[2,256,1024]{2,1,0:T(8,128)} %shard_map.129, s32[]{:T(128)S(6)} %select_n.10), kind=kLoop, calls=%fused_computation.12 | loop fusion | bytes 1048580 | tf_op jit(solution)/shard_map/convert_element_type | solution.py:386
  127.3 1.5 collective-permute-start.1
  128.8 6.5 %fusion.terms_ref = f32[2,256,2048]{2,1,0:T(8,128)} fusion(bf16[2,256,1024]{2,1,0:T(8,128)(2,1)S(1)} %copy-done.11, bf16[1024,2048]{1,0:T(8,128)(2,1)} %param.20), kind=kOutput, calls=%fused_computation | convolution fusion | flops 2147483648 | bytes 9437184 | tf_op jit(solution)/shard_map/dot_general | solution.py:20
  135.3 4.1 %shard_map.126 = f32[2,256,1024]{2,1,0:T(8,128)} custom-call(f32[2,256,2048]{2,1,0:T(8,128)} %fusion.terms_ref), custom_call_target="tpu_custom_call" | custom-call | tf_op jit(solution)/shard_map/pallas_call | solution.py:377
  139.4 2.1 %fusion.4 = bf16[256,1024]{1,0:T(8,128)(2,1)} fusion(f32[2,256,1024]{2,1,0:T(8,128)} %shard_map.126, s32[]{:T(128)S(6)} %select_n.10), kind=kLoop, calls=%fused_computation.11 | loop fusion | bytes 1048580 | tf_op jit(solution)/shard_map/convert_element_type | solution.py:386
  143.0 12.4 %collective-permute-done = bf16[256,1024]{1,0:T(8,128)(2,1)S(1)} collective-permute-done((bf16[256,1024]{1,0:T(8,128)(2,1)}, bf16[256,1024]{1,0:T(8,128)(2,1)S(1)}, u32[]{:S(2)}, u32[]{:S(2)}) %collective-permute-start) | collective-permute-done | bytes 524320 | tf_op jit(solution)/shard_map/ppermute | solution.py:387
  155.4 2.2 %fusion.3 = bf16[256,1024]{1,0:T(8,128)(2,1)} fusion(bf16[256,1024]{1,0:T(8,128)(2,1)S(1)} %collective-permute-done, f32[2,256,1024]{2,1,0:T(8,128)} %shard_map.126, s32[]{:T(128)S(6)} %select_n.9), kind=kLoop, calls=%fused_computation.8 | loop fusion | flops 786432 | bytes 2097156 | tf_op jit(solution)/shard_map/convert_element_type | solution.py:390
  (28 shorter events, 2.9 us)
Async XLA Ops:
  8.9 6.3 %copy-start.10 = (bf16[2,256,2048]{2,1,0:T(8,128)(2,1)S(1)}, bf16[2,256,2048]{2,1,0:T(8,128)(2,1)}, u32[]{:S(2)}) copy-start(bf16[2,256,2048]{2,1,0:T(8,128)(2,1)} %get-tuple-element.9) | copy-start | bytes 6291460
  8.9 7.8 %copy-start.6 = (f32[8]{0:T(128)S(1)}, f32[8]{0:T(128)}, u32[]{:S(2)}) copy-start(f32[8]{0:T(128)} %param.18) | copy-start | bytes 100
  8.9 7.8 %copy-start.7 = (f32[8]{0:T(128)S(1)}, f32[8]{0:T(128)}, u32[]{:S(2)}) copy-start(f32[8]{0:T(128)} %param.17) | copy-start | bytes 100
  8.9 7.8 %copy-start.8 = (f32[8]{0:T(128)S(1)}, f32[8]{0:T(128)}, u32[]{:S(2)}) copy-start(f32[8]{0:T(128)} %param.16) | copy-start | bytes 100
  15.2 34.2 %copy-start.9 = (bf16[2,256,2048]{2,1,0:T(8,128)(2,1)S(1)}, bf16[2,256,2048]{2,1,0:T(8,128)(2,1)}, u32[]{:S(2)}) copy-start(bf16[2,256,2048]{2,1,0:T(8,128)(2,1)} %get-tuple-element.10) | copy-start | bytes 6291460
  20.9 1.0 copy-start
  49.4 5.8 %copy-start.1 = (bf16[16,2,2,16,128]{4,3,2,1,0:T(8,128)(2,1)}, bf16[16,2,2,16,128]{4,3,2,1,0:T(8,128)(2,1)S(1)}, u32[]{:S(2)}) copy-start(bf16[16,2,2,16,128]{4,3,2,1,0:T(8,128)(2,1)S(1)} %shard_map.124.start_ref) | copy-start | bytes 786436
  69.8 1.0 copy-start.3
  93.4 0.7 copy-start.2
  113.4 4.9 %copy-start.5 = (bf16[2,256,128]{2,1,0:T(8,128)(2,1)S(1)}, bf16[2,256,128]{2,1,0:T(8,128)(2,1)}, u32[]{:S(2)}) copy-start(bf16[2,256,128]{2,1,0:T(8,128)(2,1)} %get-tuple-element.15) | copy-start | bytes 393220
  121.2 7.7 %copy-start.11 = (bf16[2,256,1024]{2,1,0:T(8,128)(2,1)S(1)}, bf16[2,256,1024]{2,1,0:T(8,128)(2,1)}, u32[]{:S(2)}) copy-start(bf16[2,256,1024]{2,1,0:T(8,128)(2,1)} %get-tuple-element.11) | copy-start | bytes 3145732
  127.3 14.7 %collective-permute-start.1 = (bf16[256,1024]{1,0:T(8,128)(2,1)}, bf16[256,1024]{1,0:T(8,128)(2,1)S(1)}, u32[]{:S(2)}, u32[]{:S(2)}) collective-permute-start(bf16[256,1024]{1,0:T(8,128)(2,1)} %fusion.5), channel_id=1, source_target_pairs={{0,1},{1,0},{2,3},{3,2},{4,5},{5,4},{6,7},{7,6},{8,9},{9,8},{10,11... | collective-permute-start | bytes 1572872 | tf_op jit(solution)/shard_map/ppermute | solution.py:387
  135.3 6.7 %copy-start.4 = (f32[2,256,1024]{2,1,0:T(8,128)S(1)}, f32[2,256,1024]{2,1,0:T(8,128)}, u32[]{:S(2)}) copy-start(f32[2,256,1024]{2,1,0:T(8,128)} %shard_map.129) | copy-start | bytes 6291460
  141.5 13.9 %collective-permute-start = (bf16[256,1024]{1,0:T(8,128)(2,1)}, bf16[256,1024]{1,0:T(8,128)(2,1)S(1)}, u32[]{:S(2)}, u32[]{:S(2)}) collective-permute-start(bf16[256,1024]{1,0:T(8,128)(2,1)} %fusion.4), channel_id=1, source_target_pairs={{0,1},{1,0},{2,3},{3,2},{4,5},{5,4},{6,7},{7,6},{8,9},{9,8},{10,11... | collective-permute-start | bytes 1572872 | tf_op jit(solution)/shard_map/ppermute | solution.py:387

commit v2 on v1

--- a/solution.py
+++ b/solution.py
@@ -42,17 +42,14 @@
         grad_ref[1, :, there] = dot(tile, mirror).astype(bf16)
 
 
-def merge_kernel(terms_ref, out_ref):
-    parts, _, width = out_ref.shape
-    tiles = parts * width // LANES
-    per = width // LANES
+def merge_kernel(main_ref, mirrored_ref, out_ref):
+    tiles = out_ref.shape[1] // LANES
     mirror = exchange_matrix()
     for k in range(tiles):
-        back = tiles - 1 - k
-        flipped = dot(terms_ref[1, :, pl.ds(back * LANES, LANES)].astype(bf16), mirror)
-        out_ref[k // per, :, pl.ds((k % per) * LANES, LANES)] = (
-            terms_ref[0, :, pl.ds(k * LANES, LANES)] + flipped
-        )
+        here = pl.ds(k * LANES, LANES)
+        there = pl.ds((tiles - 1 - k) * LANES, LANES)
+        flipped = dot(mirrored_ref[:, there].astype(bf16), mirror)
+        out_ref[:, here] = (main_ref[:, here] + flipped).astype(out_ref.dtype)
 
 
 def prepare(aux, consts):
@@ -76,11 +73,10 @@
     count, _, _, rows, _ = parcel_ref.shape
     per = count // heads
     wide = jnp.broadcast_to(decay, (rows, LANES))
-    main = wide.astype(bf16)
-    rest = (wide - main.astype(f32)).astype(bf16)
+    main = wide.astype(bf16).astype(f32)
+    packed = jnp.where(iota2((rows, LANES), 0) < rows // 2, main, wide - main).astype(bf16)
     for k in range(per):
-        parcel_ref[h * per + k, 0, 2] = main
-        parcel_ref[h * per + k, 0, 3] = rest
+        parcel_ref[h * per + k, 0, 2] = packed
 
 
 def take_rows(parcel_ref, h, heads, which):
@@ -149,7 +145,8 @@
             j = count - 1 - i if (which == 1) != upward else i
             total = totals[which]
             back[j, :, which] = total.astype(bf16)
-            decay = got[j, :, 2].astype(f32) + got[j, :, 3].astype(f32)
+            packed = got[j, :, 2].astype(f32)
+            decay = packed[:, :1] + packed[:, rows // 2 : rows // 2 + 1]
             result.append(decay * total + got[j, :, which].astype(f32))
         return tuple(result)
 
@@ -372,22 +369,31 @@
     return jax.ShapeDtypeStruct(shape, dtype)
 
 
-def join_halves(terms, parts):
-    _, length, width = terms.shape
-    halves = pl.pallas_call(
-        merge_kernel,
-        out_shape=shape_of(f32, parts, length, width // parts),
-        compiler_params=PARAMS,
-    )(terms)
-    mine = lax.axis_index("mp")
-    own = lax.dynamic_index_in_dim(halves, mine, 0, keepdims=False)
-    for hop in range(1, parts):
-        there = lax.rem(mine + hop, parts)
-        leaving = lax.dynamic_index_in_dim(halves, there, 0, keepdims=False).astype(bf16)
-        own += lax.ppermute(
-            leaving, "mp", [(i, (i + hop) % parts) for i in range(parts)]
-        ).astype(f32)
-    return own.astype(bf16)
+def merge(main, mirrored, dtype):
+    return pl.pallas_call(
+        merge_kernel, out_shape=shape_of(dtype, *main.shape), compiler_params=PARAMS
+    )(main, mirrored)
+
+
+def out_share(z, w_out, part, parts, dtype):
+    width = w_out.shape[1] // parts
+    main = lax.dynamic_slice_in_dim(w_out, part * width, width, 1)
+    mirrored = lax.dynamic_slice_in_dim(w_out, (parts - 1 - part) * width, width, 1)
+    return merge(dot(z[0], main), dot(z[1], mirrored), dtype)
+
+
+def hidden_share(dx, tail, w_value, w_side, part, parts, dtype):
+    width = w_value.shape[0] // parts
+    terms = []
+    for stream, place in ((0, part), (1, parts - 1 - part)):
+        value = lax.dynamic_slice_in_dim(w_value, place * width, width, 0)
+        side = lax.dynamic_slice_in_dim(w_side, place * width, width, 0)
+        terms.append(dot(dx[stream], value, MXU_NT) + dot(tail[stream], side, MXU_NT))
+    return merge(*terms, dtype)
+
+
+def send_on(leaving, hop, parts):
+    return lax.ppermute(leaving, "mp", [(i, (i + hop) % parts) for i in range(parts)])
 
 
 def per_device(
@@ -415,12 +421,12 @@
     x = dot(sources, w_value).astype(bf16).reshape(2, length, inner)
     assert count % heads == 0 and (heads * state) % count == 0
     rows = heads * state // count
-    parcel = (count, 2, 4, rows, LANES)
+    parcel = (count, 2, 3, rows, LANES)
     states = pl.pallas_call(
         partial(ends_kernel, heads, state),
         grid=(2,),
         in_specs=[by_stream(length, LANES), shared(8, LANES), by_stream(length, inner)],
-        out_specs=gathered(count, 4, rows, LANES),
+        out_specs=gathered(count, 3, rows, LANES),
         out_shape=shape_of(bf16, *parcel),
         compiler_params=PARAMS,
     )(aux, consts, x)
@@ -435,7 +441,7 @@
         ],
         out_specs=[
             by_stream(length, inner), by_stream(2, length, inner),
-            gathered(count, 4, rows, LANES),
+            gathered(count, 3, rows, LANES),
         ],
         out_shape=(
             shape_of(bf16, 2, length, inner), shape_of(bf16, 2, 2, length, inner),
@@ -444,8 +450,11 @@
         scratch_shapes=[pltpu.VMEM((2, length, inner), f32)],
         compiler_params=PARAMS,
     )(aux, consts, x, dz, norm_gain[None], starts)
-    out_terms = dot(z.reshape(2 * length, inner), w_out).reshape(2, length, width)
-    out = join_halves(out_terms, parts)
+    mine = lax.axis_index("mp")
+    hops = range(1, parts)
+    leaving = [out_share(z, w_out, lax.rem(mine + hop, parts), parts, bf16) for hop in hops]
+    adjoint, leaving = lax.optimization_barrier((adjoint, leaving))
+    out_received = [send_on(share, hop, parts) for hop, share in zip(hops, leaving)]
     arriving = exchange(adjoint, True, 1)
     dx, tail = pl.pallas_call(
         partial(grads_kernel, heads, state),
@@ -453,16 +462,30 @@
         in_specs=[
             by_stream(length, LANES), shared(8, LANES), by_stream(length, inner),
             by_stream(2, length, inner), gathered(count, 2, rows, LANES),
-            gathered(count, 4, rows, LANES), gathered(count, 2, rows, LANES),
+            gathered(count, 3, rows, LANES), gathered(count, 2, rows, LANES),
         ],
         out_specs=[by_stream(length, inner), by_stream(length, LANES)],
         out_shape=(shape_of(bf16, 2, length, inner), shape_of(bf16, 2, length, LANES)),
+        cost_estimate=pl.CostEstimate(
+            flops=24 * length * length * inner, bytes_accessed=16 * length * inner,
+            transcendentals=2 * heads * length * length,
+        ),
         compiler_params=PARAMS,
     )(aux, consts, x, dy, starts, states, arriving)
-    terms = dot(dx.reshape(2 * length, inner), w_value, MXU_NT)
-    terms += dot(tail.reshape(2 * length, LANES), w_side, MXU_NT)
-    d_hidden = join_halves(terms.reshape(2, length, width), parts)
-    return (out, d_hidden)
+    dx, tail, out_received = lax.optimization_barrier((dx, tail, out_received))
+    leaving = [
+        hidden_share(dx, tail, w_value, w_side, lax.rem(mine + hop, parts), parts, bf16)
+        for hop in hops
+    ]
+    dx, tail, z, leaving = lax.optimization_barrier((dx, tail, z, leaving))
+    received = [send_on(share, hop, parts) for hop, share in zip(hops, leaving)]
+    out = out_share(z, w_out, mine, parts, f32)
+    d_hidden = hidden_share(dx, tail, w_value, w_side, mine, parts, f32)
+    for share in out_received:
+        out += share.astype(f32)
+    for share in received:
+        d_hidden += share.astype(f32)
+    return (out.astype(bf16), d_hidden.astype(bf16))
 
 
 def solution(mesh):

time: 158 us -> 145 us (0.918)
  waiting for transfers between devices: 12.4 us -> 1.68 us
  matrix products: 27.8 us -> 33.2 us
  local copies, waits for them, and re-layouts: 10.8 us -> 6.73 us
  Pallas kernels: 100 us -> 96 us
    ppermute x2, waiting for transfers between devices: 12.4 us -> 1.68 us  [send_on(): lax.ppermute(leaving, 'mp', [(i, (i + hop) % parts) for i in range(parts)])]
    pallas_call x2, Pallas kernels: 49.9 us -> 42.4 us  [exchange(): pl.pallas_call(partial(exchange_kernel, upward), in_specs=[pl.BlockSpec(m...]
    dot_general x6 -> x15, matrix products: 27.8 us -> 33.2 us  [dot(): lax.dot_general(a, b, dims, preferred_element_type=f32, precision=precision)]
    convert_element_type x2 -> x0, local copies, waits for them, and re-layouts: 4.19 us -> none  [join_halves(): lax.dynamic_index_in_dim(halves, there, 0, keepdims=False).astype(bf16)]
    pallas_call x2 -> x4, Pallas kernels: 8.17 us -> 11.1 us  [merge(): pl.pallas_call(merge_kernel, out_shape=shape_of(dtype, *main.shape), comp...]
    unnamed x26 -> x38, local copies, waits for them, and re-layouts: 5.06 us -> 5.17 us
  transfers between devices with their start and end apart: 2 -> 2, of which waited for: 1 -> 1; matrix products, arithmetic and copies ran while one was open for 6% -> 4% of each run, Pallas kernels for 3% -> 32%
where the time goes in v2:
time: 145 us; the launch traced here: 144 us
  Pallas kernels  96 us (66%)
  matrix products  33.2 us (23%)
  local copies, waits for them, and re-layouts  6.73 us (5%)
  other arithmetic  4.03 us (3%)
  starting transfers between devices  2.03 us (1%)
  waiting for transfers between devices  1.68 us (1%)
    pallas_call x2, Pallas kernels, exchange(): pl.pallas_call(partial(exchange_kernel, upward), in_specs=[pl.BlockSpec(m...  42.4 us
    dot_general x15, matrix products, dot(): lax.dot_general(a, b, dims, preferred_element_type=f32, precision=precision)  33.2 us
    pallas_call x1, Pallas kernels, per_device(): pl.pallas_call(partial(grads_kernel, heads, state), grid=(2,), in_specs=[...  19.7 us
    pallas_call x1, Pallas kernels, per_device(): pl.pallas_call(partial(outputs_kernel, heads, state), grid=(2,), in_specs...  14.6 us
    pallas_call x4, Pallas kernels, merge(): pl.pallas_call(merge_kernel, out_shape=shape_of(dtype, *main.shape), comp...  11.1 us
    unnamed x38, local copies, waits for them, and re-layouts  5.17 us
    pallas_call x1, Pallas kernels, per_device(): pl.pallas_call(sources_kernel, out_shape=(shape_of(bf16, 2, length, width...  4.63 us
    pallas_call x1, Pallas kernels, per_device(): pl.pallas_call(partial(ends_kernel, heads, state), grid=(2,), in_specs=[b...  3.56 us
  transfers between devices with their start and end apart: 2, of which 1 were waited for; matrix products, arithmetic and copies ran while one was open for 4% of the time, Pallas kernels for 32%

profile of v2, /device:TPU:0, one launch (start us, length us, event | category | flops | bytes accessed | tf_op | source)
XLA Modules:
  0.0 144.4 jit_solution(18221209394790532006)
XLA Ops:
  4.8 4.6 %shard_map.122 = (bf16[2,256,2048]{2,1,0:T(8,128)(2,1)}, bf16[2,256,2048]{2,1,0:T(8,128)(2,1)}) custom-call(bf16[256,2048]{1,0:T(8,128)(2,1)} %hidden_ref.1, bf16[256,2048]{1,0:T(8,128)(2,1)} %cot_ref.1, s32[256,1]{1,0:T(8,128)} %copy.15.ids_ref), custom_call_target="tpu_custom_call" | custom-call | tf_op jit(solution)/shard_map/pallas_call | solution.py:408
  9.4 3.0 %fusion.36.aux_ref = f32[2,256,128]{2,1,0:T(8,128)} fusion(bf16[2,256,2048]{2,1,0:T(8,128)(2,1)} %get-tuple-element.18, bf16[2048,128]{1,0:T(8,128)(2,1)S(1)} %pad_maximum_fusion), kind=kOutput, calls=%fused_computation.33 | convolution fusion | flops 268435456 | bytes 2883584 | tf_op jit(solution)/shard_map/dot_general | solution.py:20
  12.5 5.1 %convolution_convert_fusion.1 = bf16[512,1024]{1,0:T(8,128)(2,1)} fusion(bf16[512,2048]{1,0:T(8,128)(2,1)} %bitcast.57, bf16[2048,1024]{1,0:T(8,128)(2,1)S(1)} %copy-done.4), kind=kOutput, calls=%fused_computation.17 | convolution fusion | flops 2148007936 | bytes 7340032 | tf_op jit(solution)/shard_map/dot_general | solution.py:20
  18.2 3.6 %shard_map.123.parcel_ref.own_ref = bf16[16,2,3,16,128]{4,3,2,1,0:T(8,128)(2,1)} custom-call(f32[2,256,128]{2,1,0:T(8,128)} %fusion.36.aux_ref, f32[8,128]{1,0:T(8,128)} %select_maximum_fusion.consts_ref, bf16[2,256,1024]{2,1,0:T(8,128)(2,1)} %bitcast.54), custom_call_target="tpu_custom_call" | custom-call | tf_op jit(solution)/shard_map/pallas_call | solution.py:425
  22.7 21.7 %shard_map.124.start_ref = bf16[16,2,2,16,128]{4,3,2,1,0:T(8,128)(2,1)S(1)} custom-call(bf16[16,2,3,16,128]{4,3,2,1,0:T(8,128)(2,1)S(1)} %copy-done), custom_call_target="tpu_custom_call" | custom-call | tf_op jit(solution)/shard_map/pallas_call | solution.py:163
  45.1 5.7 %convolution_convert_fusion = bf16[512,1024]{1,0:T(8,128)(2,1)} fusion(bf16[512,2048]{1,0:T(8,128)(2,1)S(1)} %bitcast.65, bf16[1024,2048]{1,0:T(8,128)(2,1)} %param.20), kind=kOutput, calls=%fused_computation.16 | convolution fusion | flops 2148007936 | bytes 7340032 | tf_op jit(solution)/shard_map/dot_general | solution.py:20
  50.8 14.6 %shard_map.125 = (bf16[2,256,1024]{2,1,0:T(8,128)(2,1)}, bf16[2,2,256,1024]{3,2,1,0:T(8,128)(2,1)}, bf16[16,2,3,16,128]{4,3,2,1,0:T(8,128)(2,1)}) custom-call(f32[2,256,128]{2,1,0:T(8,128)} %fusion.36.aux_ref, f32[8,128]{1,0:T(8,128)} %select_maximum_fusion.consts_ref, bf16[2,256,1024]{2,1,0:T(8,128)(2,1)} %bitcast.55, bf16[2,256,1024]{2,1,0:T(8,128)(2,1)} %bitcast.59, ...), custom_call_target="tpu_custom_call" | custom-call | tf_op jit(solution)/shard_map/pallas_call | solution.py:435
  65.4 2.8 %fusion.12.mirrored_ref = f32[256,1024]{1,0:T(8,128)} fusion(bf16[1024,2048]{1,0:T(8,128)(2,1)S(1)} %copy-done.6, s32[]{:T(128)S(6)} %select_n.9, bf16[2,256,1024]{2,1,0:T(8,128)(2,1)} %get-tuple-element.29), kind=kOutput, calls=%fused_computation.12 | convolution fusion | flops 536870912 | bytes 3670020 | tf_op jit(solution)/shard_map/dot_general | solution.py:20
  68.2 3.3 %fusion.14.main_ref = f32[256,1024]{1,0:T(8,128)} fusion(bf16[1024,2048]{1,0:T(8,128)(2,1)} %param.20, s32[]{:T(128)S(6)} %select_n.8, bf16[2,256,1024]{2,1,0:T(8,128)(2,1)S(1)} %copy-done.11), kind=kOutput, calls=%fused_computation.14 | convolution fusion | flops 536870912 | bytes 3670020 | tf_op jit(solution)/shard_map/dot_general | solution.py:20
  71.5 2.7 %shard_map.126 = bf16[256,1024]{1,0:T(8,128)(2,1)} custom-call(f32[256,1024]{1,0:T(8,128)} %fusion.14.main_ref, f32[256,1024]{1,0:T(8,128)} %fusion.12.mirrored_ref), custom_call_target="tpu_custom_call" | custom-call | tf_op jit(solution)/shard_map/pallas_call | solution.py:373
  74.2 1.5 %collective-permute-start = (bf16[256,1024]{1,0:T(8,128)(2,1)}, bf16[256,1024]{1,0:T(8,128)(2,1)S(1)}, u32[]{:S(2)}, u32[]{:S(2)}) collective-permute-start(bf16[256,1024]{1,0:T(8,128)(2,1)} %shard_map.126), channel_id=1, source_target_pairs={{0,1},{1,0},{2,3},{3,2},{4,5},{5,4},{6,7},{7,6},{8,9},{9,8},{10,11... | collective-permute-start | bytes 1572872 | tf_op jit(solution)/shard_map/ppermute | solution.py:396
  75.7 20.7 %shard_map.127.in_ref = bf16[16,2,2,16,128]{4,3,2,1,0:T(8,128)(2,1)S(1)} custom-call(bf16[16,2,3,16,128]{4,3,2,1,0:T(8,128)(2,1)S(1)} %copy-done.2), custom_call_target="tpu_custom_call" | custom-call | tf_op jit(solution)/shard_map/pallas_call | solution.py:163
  97.1 19.7 %shard_map.128 = (bf16[2,256,1024]{2,1,0:T(8,128)(2,1)}, bf16[2,256,128]{2,1,0:T(8,128)(2,1)}) custom-call(f32[2,256,128]{2,1,0:T(8,128)} %fusion.36.aux_ref, f32[8,128]{1,0:T(8,128)} %select_maximum_fusion.consts_ref, bf16[2,256,1024]{2,1,0:T(8,128)(2,1)} %bitcast.56, bf16[2,2,256,1024]{3,2,1,0:T(8,128)(2,1)} %get-tuple-element.20.dy_ref, ...), custom_call_target="tpu_custom_call" | custom-call | flops 1610612736 | bytes 4194304 | tf_op jit(solution)/shard_map/pallas_call | solution.py:459
  119.3 1.7 %fusion.19.mirrored_ref = f32[256,1024]{1,0:T(8,128)} fusion(f32[256,1024]{1,0:T(8,128)S(1)} %fusion.50, bf16[2048,1024]{1,0:T(8,128)(2,1)S(1)} %copy-done.5, s32[]{:T(128)S(6)} %select_n.9, bf16[2,256,1024]{2,1,0:T(8,128)(2,1)S(1)} %copy-done.9), kind=kOutput, calls=%fused_computation.19 | convolution fusion | flops 537133056 | bytes 4718596 | tf_op jit(solution)/shard_map/dot_general | solution.py:20
  121.0 1.8 %fusion.16.main_ref = f32[256,1024]{1,0:T(8,128)} fusion(f32[256,1024]{1,0:T(8,128)S(1)} %fusion.52, bf16[2048,1024]{1,0:T(8,128)(2,1)S(1)} %copy-done.5, s32[]{:T(128)S(6)} %select_n.8, bf16[2,256,1024]{2,1,0:T(8,128)(2,1)S(1)} %copy-done.9), kind=kOutput, calls=%fused_computation.18 | convolution fusion | flops 537133056 | bytes 4718596 | tf_op jit(solution)/shard_map/dot_general | solution.py:20
  122.8 2.7 %shard_map.129 = bf16[256,1024]{1,0:T(8,128)(2,1)} custom-call(f32[256,1024]{1,0:T(8,128)} %fusion.16.main_ref, f32[256,1024]{1,0:T(8,128)} %fusion.19.mirrored_ref), custom_call_target="tpu_custom_call" | custom-call | tf_op jit(solution)/shard_map/pallas_call | solution.py:373
  126.0 1.7 %fusion.25.mirrored_ref = f32[256,1024]{1,0:T(8,128)} fusion(f32[256,1024]{1,0:T(8,128)S(1)} %fusion.46, bf16[2048,1024]{1,0:T(8,128)(2,1)S(1)} %copy-done.5, s32[]{:T(128)S(6)} %select_n.11, bf16[2,256,1024]{2,1,0:T(8,128)(2,1)S(1)} %copy-done.9), kind=kOutput, calls=%fused_computation.21 | convolution fusion | flops 537133056 | bytes 4718596 | tf_op jit(solution)/shard_map/dot_general | solution.py:20
  127.8 1.7 %fusion.22.main_ref = f32[256,1024]{1,0:T(8,128)} fusion(f32[256,1024]{1,0:T(8,128)S(1)} %fusion.48, bf16[2048,1024]{1,0:T(8,128)(2,1)S(1)} %copy-done.5, s32[]{:T(128)S(6)} %select_n.10, bf16[2,256,1024]{2,1,0:T(8,128)(2,1)S(1)} %copy-done.9), kind=kOutput, calls=%fused_computation.20 | convolution fusion | flops 537133056 | bytes 4718596 | tf_op jit(solution)/shard_map/dot_general | solution.py:20
  130.5 1.7 %fusion.4.mirrored_ref = f32[256,1024]{1,0:T(8,128)} fusion(bf16[1024,2048]{1,0:T(8,128)(2,1)S(1)} %copy-done.7, s32[]{:T(128)S(6)} %select_n.11, bf16[2,256,1024]{2,1,0:T(8,128)(2,1)S(1)} %copy-done.11), kind=kOutput, calls=%fused_computation.4 | convolution fusion | flops 536870912 | bytes 3670020 | tf_op jit(solution)/shard_map/dot_general | solution.py:20
  132.2 2.8 %shard_map.131 = f32[256,1024]{1,0:T(8,128)} custom-call(f32[256,1024]{1,0:T(8,128)} %fusion.22.main_ref, f32[256,1024]{1,0:T(8,128)} %fusion.25.mirrored_ref), custom_call_target="tpu_custom_call" | custom-call | tf_op jit(solution)/shard_map/pallas_call | solution.py:373
  135.1 1.7 %fusion.6.main_ref = f32[256,1024]{1,0:T(8,128)} fusion(bf16[1024,2048]{1,0:T(8,128)(2,1)S(1)} %copy-done.8, s32[]{:T(128)S(6)} %select_n.10, bf16[2,256,1024]{2,1,0:T(8,128)(2,1)S(1)} %copy-done.11), kind=kOutput, calls=%fused_computation.6 | convolution fusion | flops 536870912 | bytes 3670020 | tf_op jit(solution)/shard_map/dot_general | solution.py:20
  136.7 2.9 %shard_map.130 = f32[256,1024]{1,0:T(8,128)} custom-call(f32[256,1024]{1,0:T(8,128)} %fusion.6.main_ref, f32[256,1024]{1,0:T(8,128)} %fusion.4.mirrored_ref), custom_call_target="tpu_custom_call" | custom-call | tf_op jit(solution)/shard_map/pallas_call | solution.py:373
  139.6 2.2 %add_convert_fusion.1 = bf16[256,1024]{1,0:T(8,128)(2,1)} fusion(f32[256,1024]{1,0:T(8,128)} %shard_map.130, bf16[256,1024]{1,0:T(8,128)(2,1)S(1)} %collective-permute-done), kind=kLoop, calls=%fused_computation.23 | loop fusion | flops 786432 | bytes 2097152 | tf_op jit(solution)/shard_map/convert_element_type | solution.py:488
  141.8 1.7 %collective-permute-done.1 = bf16[256,1024]{1,0:T(8,128)(2,1)S(1)} collective-permute-done((bf16[256,1024]{1,0:T(8,128)(2,1)S(1)}, bf16[256,1024]{1,0:T(8,128)(2,1)S(1)}, u32[]{:S(2)}, u32[]{:S(2)}) %collective-permute-start.1) | collective-permute-done | bytes 524320 | tf_op jit(solution)/shard_map/ppermute | solution.py:396
  (50 shorter events, 12.1 us)
Async XLA Ops:
  4.8 7.7 %copy-start.4 = (bf16[2048,1024]{1,0:T(8,128)(2,1)S(1)}, bf16[2048,1024]{1,0:T(8,128)(2,1)}, u32[]{:S(2)}) copy-start(bf16[2048,1024]{1,0:T(8,128)(2,1)} %param.13) | copy-start | bytes 12582916
  12.5 5.1 %copy-start.14 = (f32[8]{0:T(128)S(1)}, f32[8]{0:T(128)}, u32[]{:S(2)}) copy-start(f32[8]{0:T(128)} %param.18) | copy-start | bytes 100
  12.5 5.1 %copy-start.15 = (f32[8]{0:T(128)S(1)}, f32[8]{0:T(128)}, u32[]{:S(2)}) copy-start(f32[8]{0:T(128)} %param.17) | copy-start | bytes 100
  12.5 5.1 %copy-start.16 = (f32[8]{0:T(128)S(1)}, f32[8]{0:T(128)}, u32[]{:S(2)}) copy-start(f32[8]{0:T(128)} %param.16) | copy-start | bytes 100
  12.5 32.7 %copy-start.17 = (bf16[2,256,2048]{2,1,0:T(8,128)(2,1)S(1)}, bf16[2,256,2048]{2,1,0:T(8,128)(2,1)}, u32[]{:S(2)}) copy-start(bf16[2,256,2048]{2,1,0:T(8,128)(2,1)} %get-tuple-element.19) | copy-start | bytes 6291460
  21.7 1.0 copy-start
  44.4 0.7 copy-start.1
  45.1 20.3 %copy-start.6 = (bf16[1024,2048]{1,0:T(8,128)(2,1)S(1)}, bf16[1024,2048]{1,0:T(8,128)(2,1)}, u32[]{:S(2)}) copy-start(bf16[1024,2048]{1,0:T(8,128)(2,1)} %param.20) | copy-start | bytes 12582916
  65.4 2.8 %copy-start.11 = (bf16[2,256,1024]{2,1,0:T(8,128)(2,1)S(1)}, bf16[2,256,1024]{2,1,0:T(8,128)(2,1)}, u32[]{:S(2)}) copy-start(bf16[2,256,1024]{2,1,0:T(8,128)(2,1)} %get-tuple-element.29) | copy-start | bytes 3145732
  71.5 4.2 %copy-start.2 = (bf16[16,2,3,16,128]{4,3,2,1,0:T(8,128)(2,1)S(1)}, bf16[16,2,3,16,128]{4,3,2,1,0:T(8,128)(2,1)}, u32[]{:S(2)}) copy-start(bf16[16,2,3,16,128]{4,3,2,1,0:T(8,128)(2,1)} %get-tuple-element.23.parcel_ref) | copy-start | bytes 1179652
  74.2 42.7 %collective-permute-start = (bf16[256,1024]{1,0:T(8,128)(2,1)}, bf16[256,1024]{1,0:T(8,128)(2,1)S(1)}, u32[]{:S(2)}, u32[]{:S(2)}) collective-permute-start(bf16[256,1024]{1,0:T(8,128)(2,1)} %shard_map.126), channel_id=1, source_target_pairs={{0,1},{1,0},{2,3},{3,2},{4,5},{5,4},{6,7},{7,6},{8,9},{9,8},{10,11... | collective-permute-start | bytes 1572872 | tf_op jit(solution)/shard_map/ppermute | solution.py:396
  96.4 0.7 copy-start.3
  97.1 22.1 %copy-start.5 = (bf16[2048,1024]{1,0:T(8,128)(2,1)S(1)}, bf16[2048,1024]{1,0:T(8,128)(2,1)}, u32[]{:S(2)}) copy-start(bf16[2048,1024]{1,0:T(8,128)(2,1)} %param.13) | copy-start | bytes 12582916
  116.9 2.4 %copy-start.9 = (bf16[2,256,1024]{2,1,0:T(8,128)(2,1)S(1)}, bf16[2,256,1024]{2,1,0:T(8,128)(2,1)}, u32[]{:S(2)}) copy-start(bf16[2,256,1024]{2,1,0:T(8,128)(2,1)} %get-tuple-element.31) | copy-start | bytes 3145732
  122.8 2.7 %copy-start.13 = (bf16[2,256,128]{2,1,0:T(8,128)(2,1)S(1)}, bf16[2,256,128]{2,1,0:T(8,128)(2,1)}, u32[]{:S(2)}) copy-start(bf16[2,256,128]{2,1,0:T(8,128)(2,1)} %get-tuple-element.32) | copy-start | bytes 393220
  127.8 1.7 %copy-start.12 = (bf16[256,1024]{1,0:T(8,128)(2,1)S(1)}, bf16[256,1024]{1,0:T(8,128)(2,1)}, u32[]{:S(2)}) copy-start(bf16[256,1024]{1,0:T(8,128)(2,1)} %shard_map.129) | copy-start | bytes 1572868
  127.8 2.7 %copy-start.7 = (bf16[1024,2048]{1,0:T(8,128)(2,1)S(1)}, bf16[1024,2048]{1,0:T(8,128)(2,1)}, u32[]{:S(2)}) copy-start(bf16[1024,2048]{1,0:T(8,128)(2,1)} %param.20) | copy-start | bytes 12582916
  129.5 14.0 %collective-permute-start.1 = (bf16[256,1024]{1,0:T(8,128)(2,1)S(1)}, bf16[256,1024]{1,0:T(8,128)(2,1)S(1)}, u32[]{:S(2)}, u32[]{:S(2)}) collective-permute-start(bf16[256,1024]{1,0:T(8,128)(2,1)S(1)} %copy-done.12), channel_id=1, source_target_pairs={{0,1},{1,0},{2,3},{3,2},{4,5},{5,4},{6,7},{7,6},{8,9},{9,8},{10,11... | collective-permute-start | bytes 1572872 | tf_op jit(solution)/shard_map/ppermute | solution.py:396
  130.5 4.5 %copy-start.8 = (bf16[1024,2048]{1,0:T(8,128)(2,1)S(1)}, bf16[1024,2048]{1,0:T(8,128)(2,1)}, u32[]{:S(2)}) copy-start(bf16[1024,2048]{1,0:T(8,128)(2,1)} %param.20) | copy-start | bytes 12582916
  136.7 6.7 %copy-start.10 = (f32[256,1024]{1,0:T(8,128)S(1)}, f32[256,1024]{1,0:T(8,128)}, u32[]{:S(2)}) copy-start(f32[256,1024]{1,0:T(8,128)} %shard_map.131) | copy-start | bytes 3145732
